TPU v7x, 32 devices: a whole 2x2x4 slice. The times are simulated.
32 devices in a mesh: wide: 8 (over y, x, core), narrow: 4 (over z).
Axes of the slice: x: 2, y: 2, z: 4, core: 2. Of those that a mesh axis runs over, the one named last changes fastest.
Arguments:
- source_features: float32 [50, 16384], P(None, ('wide', 'narrow')), may hold values from -24 to 24
- target_features: float32 [50, 65536], P(None, 'narrow'), may hold values from -24 to 24
- source_mass: float32 [16384], P('wide'), may hold values from 0.05 to 20
- target_mass: float32 [65536], P('narrow'), may hold values from 0.05 to 20
- block_cols: int32 [128, 32], P('wide', 'narrow'), may hold values from 0 to 127, as said below
- block_counts: int32 [128, 4], P('wide', 'narrow'), may hold values from 1 to 8, as said below
Outputs:
- row_potential: float32 [16384], P('wide')
- col_potential: float32 [65536], P('narrow')
Inputs may be any that keep to these rules, and one draw needn't show every extreme that they name: `block_cols`: each list of 8 entries holds distinct column tile ids of its group; every column tile of every group is the first entry of some row tile's list. `block_counts`: on the 16 row tiles of one index of wide and one column group the counts sum to at most 96, and to exactly 96 on some such device.
All inputs are finite; a program needn't handle non-finite values.
Results may differ from a plain program's by a relative error of at most 0.0003.
Values sent between devices are 32-bit elements; how exact they have to be, the bound alone decides.
A program may use at most 64 MiB of HBM per device.

v0:
```python
import jax
import jax.numpy as jnp
from jax import lax
from jax.sharding import PartitionSpec as P

F = 50
TILE = 128
K_MAX = 8
ITERS = 2


epsilon = 0.05
very_low = -1e30


def combined_all(shard, axis, combine):
    everything = jax.tree.map(lambda part: lax.all_gather(part, axis), shard)
    leading = jax.tree.map(lambda part: part[0], everything)

    def turn(k, so_far):
        return combine(so_far, jax.tree.map(lambda part: part[k], everything))

    return lax.fori_loop(1, lax.axis_size(axis), turn, leading)


def combine(left_part, right_part):
    highest = jnp.maximum(left_part[0], right_part[0])
    summed = left_part[1] * jnp.exp(left_part[0] - highest) + right_part[1] * jnp.exp(
        right_part[0] - highest
    )
    return (highest, summed)


def fold_into(running, belongs, peaks, masses):
    highest, summed = running
    newest = jnp.max(jnp.where(belongs[:, :, None], peaks[None], very_low), axis=1)
    new_high = jnp.maximum(highest, newest)
    addition = jnp.sum(
        jnp.where(
            belongs[:, :, None], masses[None] * jnp.exp(peaks[None] - new_high[:, None, :]), 0.0
        ),
        axis=1,
    )
    return (new_high, summed * jnp.exp(highest - new_high) + addition)


def local(source_features, target_features, source_mass, target_mass, block_cols, block_counts):
    sources = lax.all_gather(source_features, "narrow", axis=1, tiled=True)
    row_count = sources.shape[1] // TILE
    col_count = target_features.shape[1] // TILE
    source_tiles = sources.reshape(F, row_count, TILE)
    target_tiles = target_features.reshape(F, col_count, TILE)
    source_norm = jnp.sum(sources * sources, axis=0).reshape(row_count, TILE)
    target_norm = jnp.sum(target_features * target_features, axis=0).reshape(col_count, TILE)
    tile_rows = (
        jnp.arange(row_count, dtype=jnp.int32)[:, None] + jnp.zeros((1, K_MAX), jnp.int32)
    ).reshape(-1)
    tile_cols = block_cols.reshape(-1)
    is_live = (jnp.arange(K_MAX, dtype=jnp.int32)[None, :] < block_counts).reshape(-1)
    slot_count = tile_rows.shape[0]
    group_size = 32
    slot_lists = (
        tile_rows.reshape(-1, group_size),
        tile_cols.reshape(-1, group_size),
        is_live.reshape(-1, group_size),
    )
    row_range = jnp.arange(row_count, dtype=jnp.int32)
    col_range = jnp.arange(col_count, dtype=jnp.int32)

    def cost_tiles(rows_of_slots, cols_of_slots):
        source_part = jnp.take(source_tiles, rows_of_slots, axis=1)
        target_part = jnp.take(target_tiles, cols_of_slots, axis=1)
        inner = jnp.einsum(
            "fga,fgb->gab",
            source_part,
            target_part,
            precision=lax.Precision.HIGHEST,
            preferred_element_type=jnp.float32,
        )
        return (
            source_norm[rows_of_slots][:, :, None]
            + target_norm[cols_of_slots][:, None, :]
            - 2.0 * inner
        ) / F

    def row_pass(col_tiles_values):

        def row_advance(running, slot_group):
            rows_of_slots, cols_of_slots, alive = slot_group
            scores = (
                col_tiles_values[cols_of_slots][:, None, :]
                - cost_tiles(rows_of_slots, cols_of_slots)
            ) / epsilon
            peaks = jnp.max(scores, axis=2)
            masses = jnp.sum(jnp.exp(scores - peaks[:, :, None]), axis=2)
            peaks = jnp.where(alive[:, None], peaks, very_low)
            masses = jnp.where(alive[:, None], masses, 0.0)
            belongs = (rows_of_slots[None, :] == row_range[:, None]) & alive[None, :]
            return (fold_into(running, belongs, peaks, masses), None)

        initial = (
            jnp.full((row_count, TILE), very_low, jnp.float32),
            jnp.zeros((row_count, TILE), jnp.float32),
        )
        (highest, summed), _ = lax.scan(row_advance, initial, slot_lists)
        highest, summed = combined_all((highest, summed), "narrow", combine)
        return epsilon * jnp.log(source_mass) - epsilon * (
            highest.reshape(-1) + jnp.log(summed.reshape(-1))
        )

    def col_pass(row_tiles_values):

        def col_advance(running, slot_group):
            rows_of_slots, cols_of_slots, alive = slot_group
            scores = (
                row_tiles_values[rows_of_slots][:, :, None]
                - cost_tiles(rows_of_slots, cols_of_slots)
            ) / epsilon
            peaks = jnp.max(scores, axis=1)
            masses = jnp.sum(jnp.exp(scores - peaks[:, None, :]), axis=1)
            peaks = jnp.where(alive[:, None], peaks, very_low)
            masses = jnp.where(alive[:, None], masses, 0.0)
            belongs = (cols_of_slots[None, :] == col_range[:, None]) & alive[None, :]
            return (fold_into(running, belongs, peaks, masses), None)

        initial = (
            jnp.full((col_count, TILE), very_low, jnp.float32),
            jnp.zeros((col_count, TILE), jnp.float32),
        )
        (highest, summed), _ = lax.scan(col_advance, initial, slot_lists)
        return (highest, summed)

    col_values = jnp.zeros((col_count, TILE), jnp.float32)
    row_values = jnp.zeros((row_count * TILE,), jnp.float32)
    for iteration in range(ITERS):
        row_values = row_pass(col_values)
        local_high, local_sum = col_pass(row_values.reshape(row_count, TILE))
        whole_high, whole_sum = combined_all((local_high, local_sum), "wide", combine)
        new_values = epsilon * jnp.log(target_mass) - epsilon * (
            whole_high.reshape(-1) + jnp.log(whole_sum.reshape(-1))
        )
        col_values = new_values.reshape(col_count, TILE)
    return (row_values, col_values.reshape(-1))


def solution(mesh):
    in_specs = (
        P(None, ("wide", "narrow")),
        P(None, "narrow"),
        P("wide"),
        P("narrow"),
        P("wide", "narrow"),
        P("wide", "narrow"),
    )
    out_specs = (P("wide"), P("narrow"))
    return jax.shard_map(local, mesh=mesh, in_specs=in_specs, out_specs=out_specs, check_vma=False)
```

profile of v0, /device:TPU:0, one launch (start us, length us, event | category | flops | bytes accessed | tf_op | source)
XLA Modules:
  0.0 313.2 jit_solution(14472225430437417820)
XLA Ops:
  0.6 17.0 %all_gather.51 = f32[50,2048]{1,0:T(8,128)S(1)} all-gather(f32[50,512]{1,0:T(8,128)} %param.26), channel_id=1, replica_groups=mesh['wide'=8,'narrow'=4] {'narrow'}, dimensions={1}, use_global_device_ids=true | all-gather | bytes 512000 | tf_op jit(solution)/shard_map/all_gather | solution.py:48
  18.0 2.7 copy.48
  21.0 3.7 %copy.40 = f32[50,128,128]{2,0,1:T(8,128)} copy(f32[50,128,128]{2,1,0:T(8,128)S(1)} %slice.89) | data formatting | bytes 6553600
  27.0 44.2 %while.124 = (s32[]{:T(128)}, f32[16,128]{1,0:T(8,128)S(1)}, f32[16,128]{1,0:T(8,128)S(1)}, s32[4,32]{1,0:T(4,128)S(1)}, pred[4,32]{1,0:T(4,128)(4,1)S(1)}, /*in...) while((s32[]{:T(128)}, f32[16,128]{1,0:T(8,128)S(1)}, ...), condition=%wide.region_7.10_spmd.clone, body=%wide.region_2.9_spmd.clone.sunk | while | flops 320110240 | bytes 9613720 | solution.py:105
  32.1 5.1 %fusion.103 = (f32[32,128]{1,0:T(8,128)S(1)}, f32[32,128,128]{1,2,0:T(8,128)S(1)}) fusion(f32[32,50,128]{2,1,0:T(8,128)S(1)} %gather_fusion, pred[32]{0:T(512)(128)(4,1)S(1)} %get-tuple-element.1669, f32[32,50,128]{2,1,0:T(8,128)S(1)} %gather_fusion.1, pred[32]{0:T(512)(128)(4,1)S(1)} %get-tuple-element.1671, f32[32,128]{1,0:T(8,128)S(1)} %gather_fusion.2, ...), kind=kOutput, calls=%fused_computation.196.clone.1 | convolution fusion | flops 318648320 | bytes 3801152 | tf_op jit(solution)/shard_map/while/body/eval_jaxpr/fga,fgb->gab/dot_general | solution.py:73
  43.1 5.1 %fusion.103 = (f32[32,128]{1,0:T(8,128)S(1)}, f32[32,128,128]{1,2,0:T(8,128)S(1)}) fusion(f32[32,50,128]{2,1,0:T(8,128)S(1)} %gather_fusion, pred[32]{0:T(512)(128)(4,1)S(1)} %get-tuple-element.1669, f32[32,50,128]{2,1,0:T(8,128)S(1)} %gather_fusion.1, pred[32]{0:T(512)(128)(4,1)S(1)} %get-tuple-element.1671, f32[32,128]{1,0:T(8,128)S(1)} %gather_fusion.2, ...), kind=kOutput, calls=%fused_computation.196.clone.1 | convolution fusion | flops 318648320 | bytes 3801152 | tf_op jit(solution)/shard_map/while/body/eval_jaxpr/fga,fgb->gab/dot_general | solution.py:73
  54.2 5.1 %fusion.103 = (f32[32,128]{1,0:T(8,128)S(1)}, f32[32,128,128]{1,2,0:T(8,128)S(1)}) fusion(f32[32,50,128]{2,1,0:T(8,128)S(1)} %gather_fusion, pred[32]{0:T(512)(128)(4,1)S(1)} %get-tuple-element.1669, f32[32,50,128]{2,1,0:T(8,128)S(1)} %gather_fusion.1, pred[32]{0:T(512)(128)(4,1)S(1)} %get-tuple-element.1671, f32[32,128]{1,0:T(8,128)S(1)} %gather_fusion.2, ...), kind=kOutput, calls=%fused_computation.196.clone.1 | convolution fusion | flops 318648320 | bytes 3801152 | tf_op jit(solution)/shard_map/while/body/eval_jaxpr/fga,fgb->gab/dot_general | solution.py:73
  60.8 2.6 gather_fusion
  65.3 5.1 %fusion.103 = (f32[32,128]{1,0:T(8,128)S(1)}, f32[32,128,128]{1,2,0:T(8,128)S(1)}) fusion(f32[32,50,128]{2,1,0:T(8,128)S(1)} %gather_fusion, pred[32]{0:T(512)(128)(4,1)S(1)} %get-tuple-element.1669, f32[32,50,128]{2,1,0:T(8,128)S(1)} %gather_fusion.1, pred[32]{0:T(512)(128)(4,1)S(1)} %get-tuple-element.1671, f32[32,128]{1,0:T(8,128)S(1)} %gather_fusion.2, ...), kind=kOutput, calls=%fused_computation.196.clone.1 | convolution fusion | flops 318648320 | bytes 3801152 | tf_op jit(solution)/shard_map/while/body/eval_jaxpr/fga,fgb->gab/dot_general | solution.py:73
  71.2 13.4 %all-gather = f32[64,128]{1,0:T(8,128)S(1)} all-gather(f32[16,128]{1,0:T(8,128)S(1)} %get-tuple-element.783), channel_id=2, replica_groups=mesh['wide'=8,'narrow'=4] {'narrow'}, dimensions={0}, use_global_device_ids=true | all-gather | bytes 40960 | tf_op jit(solution)/shard_map/all_gather | solution.py:17
  84.7 13.1 %all-gather.1 = f32[64,128]{1,0:T(8,128)S(1)} all-gather(f32[16,128]{1,0:T(8,128)S(1)} %get-tuple-element.784), channel_id=3, replica_groups=mesh['wide'=8,'narrow'=4] {'narrow'}, dimensions={0}, use_global_device_ids=true | all-gather | bytes 40960 | tf_op jit(solution)/shard_map/all_gather | solution.py:17
  97.9 52.0 %while.125 = (s32[]{:T(128)}, f32[128,128]{1,0:T(8,128)S(1)}, f32[128,128]{1,0:T(8,128)S(1)}, s32[4,32]{1,0:T(4,128)S(1)}, pred[4,32]{1,0:T(4,128)(4,1)S(1)}, /*...) while((s32[]{:T(128)}, f32[128,128]{1,0:T(8,128)S(1)}, ...), condition=%wide.region_15.18_spmd.clone, body=%wide.region_10.17_spmd.clone.sunk | while | flops 322941600 | bytes 10312596 | solution.py:130
  103.0 5.1 %fusion.107 = (f32[32,128]{1,0:T(8,128)S(1)}, f32[32,128,128]{2,1,0:T(8,128)S(1)}) fusion(f32[32,50,128]{2,1,0:T(8,128)S(1)} %gather_fusion.5, pred[32]{0:T(512)(128)(4,1)S(1)} %get-tuple-element.1690, f32[32,50,128]{2,1,0:T(8,128)S(1)} %gather_fusion.6, pred[32]{0:T(512)(128)(4,1)S(1)} %get-tuple-element.1692, f32[32,128]{1,0:T(8,128)S(1)} %gather_fusion.7, ...), kind=kOutput, calls=%fused_computation.197.clone.1 | convolution fusion | flops 318648320 | bytes 3801152 | tf_op jit(solution)/shard_map/while/body/eval_jaxpr/fga,fgb->gab/dot_general | solution.py:73
  116.0 5.1 %fusion.107 = (f32[32,128]{1,0:T(8,128)S(1)}, f32[32,128,128]{2,1,0:T(8,128)S(1)}) fusion(f32[32,50,128]{2,1,0:T(8,128)S(1)} %gather_fusion.5, pred[32]{0:T(512)(128)(4,1)S(1)} %get-tuple-element.1690, f32[32,50,128]{2,1,0:T(8,128)S(1)} %gather_fusion.6, pred[32]{0:T(512)(128)(4,1)S(1)} %get-tuple-element.1692, f32[32,128]{1,0:T(8,128)S(1)} %gather_fusion.7, ...), kind=kOutput, calls=%fused_computation.197.clone.1 | convolution fusion | flops 318648320 | bytes 3801152 | tf_op jit(solution)/shard_map/while/body/eval_jaxpr/fga,fgb->gab/dot_general | solution.py:73
  129.0 5.1 %fusion.107 = (f32[32,128]{1,0:T(8,128)S(1)}, f32[32,128,128]{2,1,0:T(8,128)S(1)}) fusion(f32[32,50,128]{2,1,0:T(8,128)S(1)} %gather_fusion.5, pred[32]{0:T(512)(128)(4,1)S(1)} %get-tuple-element.1690, f32[32,50,128]{2,1,0:T(8,128)S(1)} %gather_fusion.6, pred[32]{0:T(512)(128)(4,1)S(1)} %get-tuple-element.1692, f32[32,128]{1,0:T(8,128)S(1)} %gather_fusion.7, ...), kind=kOutput, calls=%fused_computation.197.clone.1 | convolution fusion | flops 318648320 | bytes 3801152 | tf_op jit(solution)/shard_map/while/body/eval_jaxpr/fga,fgb->gab/dot_general | solution.py:73
  142.0 5.1 %fusion.107 = (f32[32,128]{1,0:T(8,128)S(1)}, f32[32,128,128]{2,1,0:T(8,128)S(1)}) fusion(f32[32,50,128]{2,1,0:T(8,128)S(1)} %gather_fusion.5, pred[32]{0:T(512)(128)(4,1)S(1)} %get-tuple-element.1690, f32[32,50,128]{2,1,0:T(8,128)S(1)} %gather_fusion.6, pred[32]{0:T(512)(128)(4,1)S(1)} %get-tuple-element.1692, f32[32,128]{1,0:T(8,128)S(1)} %gather_fusion.7, ...), kind=kOutput, calls=%fused_computation.197.clone.1 | convolution fusion | flops 318648320 | bytes 3801152 | tf_op jit(solution)/shard_map/while/body/eval_jaxpr/fga,fgb->gab/dot_general | solution.py:73
  149.9 10.0 %all-gather.2 = f32[1024,128]{1,0:T(8,128)S(1)} all-gather(f32[128,128]{1,0:T(8,128)S(1)} %get-tuple-element.787), channel_id=4, replica_groups=mesh['wide'=8,'narrow'=4] {'wide'}, dimensions={0}, use_global_device_ids=true | all-gather | bytes 589824 | tf_op jit(solution)/shard_map/all_gather | solution.py:17
  159.9 10.0 %all-gather.3 = f32[1024,128]{1,0:T(8,128)S(1)} all-gather(f32[128,128]{1,0:T(8,128)S(1)} %get-tuple-element.788), channel_id=5, replica_groups=mesh['wide'=8,'narrow'=4] {'wide'}, dimensions={0}, use_global_device_ids=true | all-gather | bytes 589824 | tf_op jit(solution)/shard_map/all_gather | solution.py:17
  170.6 44.2 %while.126 = (s32[]{:T(128)}, f32[16,128]{1,0:T(8,128)S(1)}, f32[16,128]{1,0:T(8,128)S(1)}, s32[4,32]{1,0:T(4,128)S(1)}, pred[4,32]{1,0:T(4,128)(4,1)S(1)}, /*in...) while((s32[]{:T(128)}, f32[16,128]{1,0:T(8,128)S(1)}, ...), condition=%wide.region_23.26_spmd.clone, body=%wide.region_18.25_spmd.clone.sunk | while | flops 320110240 | bytes 9548180 | solution.py:105
  175.7 5.1 %fusion.111 = (f32[32,128]{1,0:T(8,128)S(1)}, f32[32,128,128]{1,2,0:T(8,128)S(1)}) fusion(f32[32,50,128]{2,1,0:T(8,128)S(1)} %gather_fusion.10, pred[32]{0:T(512)(128)(4,1)S(1)} %get-tuple-element.1711, f32[32,50,128]{2,1,0:T(8,128)S(1)} %gather_fusion.11, pred[32]{0:T(512)(128)(4,1)S(1)} %get-tuple-element.1713, f32[32,128]{1,0:T(8,128)S(1)} %gather_fusion.12, ...), kind=kOutput, calls=%fused_computation.198.clone.1 | convolution fusion | flops 318648320 | bytes 3801152 | tf_op jit(solution)/shard_map/while/body/eval_jaxpr/fga,fgb->gab/dot_general | solution.py:73
  186.8 5.1 %fusion.111 = (f32[32,128]{1,0:T(8,128)S(1)}, f32[32,128,128]{1,2,0:T(8,128)S(1)}) fusion(f32[32,50,128]{2,1,0:T(8,128)S(1)} %gather_fusion.10, pred[32]{0:T(512)(128)(4,1)S(1)} %get-tuple-element.1711, f32[32,50,128]{2,1,0:T(8,128)S(1)} %gather_fusion.11, pred[32]{0:T(512)(128)(4,1)S(1)} %get-tuple-element.1713, f32[32,128]{1,0:T(8,128)S(1)} %gather_fusion.12, ...), kind=kOutput, calls=%fused_computation.198.clone.1 | convolution fusion | flops 318648320 | bytes 3801152 | tf_op jit(solution)/shard_map/while/body/eval_jaxpr/fga,fgb->gab/dot_general | solution.py:73
  197.8 5.1 %fusion.111 = (f32[32,128]{1,0:T(8,128)S(1)}, f32[32,128,128]{1,2,0:T(8,128)S(1)}) fusion(f32[32,50,128]{2,1,0:T(8,128)S(1)} %gather_fusion.10, pred[32]{0:T(512)(128)(4,1)S(1)} %get-tuple-element.1711, f32[32,50,128]{2,1,0:T(8,128)S(1)} %gather_fusion.11, pred[32]{0:T(512)(128)(4,1)S(1)} %get-tuple-element.1713, f32[32,128]{1,0:T(8,128)S(1)} %gather_fusion.12, ...), kind=kOutput, calls=%fused_computation.198.clone.1 | convolution fusion | flops 318648320 | bytes 3801152 | tf_op jit(solution)/shard_map/while/body/eval_jaxpr/fga,fgb->gab/dot_general | solution.py:73
  208.9 5.1 %fusion.111 = (f32[32,128]{1,0:T(8,128)S(1)}, f32[32,128,128]{1,2,0:T(8,128)S(1)}) fusion(f32[32,50,128]{2,1,0:T(8,128)S(1)} %gather_fusion.10, pred[32]{0:T(512)(128)(4,1)S(1)} %get-tuple-element.1711, f32[32,50,128]{2,1,0:T(8,128)S(1)} %gather_fusion.11, pred[32]{0:T(512)(128)(4,1)S(1)} %get-tuple-element.1713, f32[32,128]{1,0:T(8,128)S(1)} %gather_fusion.12, ...), kind=kOutput, calls=%fused_computation.198.clone.1 | convolution fusion | flops 318648320 | bytes 3801152 | tf_op jit(solution)/shard_map/while/body/eval_jaxpr/fga,fgb->gab/dot_general | solution.py:73
  214.8 13.2 %all-gather.4 = f32[64,128]{1,0:T(8,128)S(1)} all-gather(f32[16,128]{1,0:T(8,128)S(1)} %get-tuple-element.791), channel_id=6, replica_groups=mesh['wide'=8,'narrow'=4] {'narrow'}, dimensions={0}, use_global_device_ids=true | all-gather | bytes 40960 | tf_op jit(solution)/shard_map/all_gather | solution.py:17
  228.0 13.1 %all-gather.5 = f32[64,128]{1,0:T(8,128)S(1)} all-gather(f32[16,128]{1,0:T(8,128)S(1)} %get-tuple-element.792), channel_id=7, replica_groups=mesh['wide'=8,'narrow'=4] {'narrow'}, dimensions={0}, use_global_device_ids=true | all-gather | bytes 40960 | tf_op jit(solution)/shard_map/all_gather | solution.py:17
  241.3 52.0 %while.127 = (s32[]{:T(128)}, f32[128,128]{1,0:T(8,128)S(1)}, f32[128,128]{1,0:T(8,128)S(1)}, s32[4,32]{1,0:T(4,128)S(1)}, pred[4,32]{1,0:T(4,128)(4,1)S(1)}, /*...) while((s32[]{:T(128)}, f32[128,128]{1,0:T(8,128)S(1)}, ...), condition=%wide.region_31.34_spmd.clone, body=%wide.region_26.33_spmd.clone.sunk | while | flops 322941600 | bytes 10312596 | solution.py:130
  246.4 5.1 %fusion.115 = (f32[32,128]{1,0:T(8,128)S(1)}, f32[32,128,128]{2,1,0:T(8,128)S(1)}) fusion(f32[32,50,128]{2,1,0:T(8,128)S(1)} %gather_fusion.15, pred[32]{0:T(512)(128)(4,1)S(1)} %get-tuple-element.1732, f32[32,50,128]{2,1,0:T(8,128)S(1)} %gather_fusion.16, pred[32]{0:T(512)(128)(4,1)S(1)} %get-tuple-element.1734, f32[32,128]{1,0:T(8,128)S(1)} %gather_fusion.17, ...), kind=kOutput, calls=%fused_computation.199.clone.1 | convolution fusion | flops 318648320 | bytes 3801152 | tf_op jit(solution)/shard_map/while/body/eval_jaxpr/fga,fgb->gab/dot_general | solution.py:73
  259.4 5.1 %fusion.115 = (f32[32,128]{1,0:T(8,128)S(1)}, f32[32,128,128]{2,1,0:T(8,128)S(1)}) fusion(f32[32,50,128]{2,1,0:T(8,128)S(1)} %gather_fusion.15, pred[32]{0:T(512)(128)(4,1)S(1)} %get-tuple-element.1732, f32[32,50,128]{2,1,0:T(8,128)S(1)} %gather_fusion.16, pred[32]{0:T(512)(128)(4,1)S(1)} %get-tuple-element.1734, f32[32,128]{1,0:T(8,128)S(1)} %gather_fusion.17, ...), kind=kOutput, calls=%fused_computation.199.clone.1 | convolution fusion | flops 318648320 | bytes 3801152 | tf_op jit(solution)/shard_map/while/body/eval_jaxpr/fga,fgb->gab/dot_general | solution.py:73
  272.4 5.1 %fusion.115 = (f32[32,128]{1,0:T(8,128)S(1)}, f32[32,128,128]{2,1,0:T(8,128)S(1)}) fusion(f32[32,50,128]{2,1,0:T(8,128)S(1)} %gather_fusion.15, pred[32]{0:T(512)(128)(4,1)S(1)} %get-tuple-element.1732, f32[32,50,128]{2,1,0:T(8,128)S(1)} %gather_fusion.16, pred[32]{0:T(512)(128)(4,1)S(1)} %get-tuple-element.1734, f32[32,128]{1,0:T(8,128)S(1)} %gather_fusion.17, ...), kind=kOutput, calls=%fused_computation.199.clone.1 | convolution fusion | flops 318648320 | bytes 3801152 | tf_op jit(solution)/shard_map/while/body/eval_jaxpr/fga,fgb->gab/dot_general | solution.py:73
  285.4 5.1 %fusion.115 = (f32[32,128]{1,0:T(8,128)S(1)}, f32[32,128,128]{2,1,0:T(8,128)S(1)}) fusion(f32[32,50,128]{2,1,0:T(8,128)S(1)} %gather_fusion.15, pred[32]{0:T(512)(128)(4,1)S(1)} %get-tuple-element.1732, f32[32,50,128]{2,1,0:T(8,128)S(1)} %gather_fusion.16, pred[32]{0:T(512)(128)(4,1)S(1)} %get-tuple-element.1734, f32[32,128]{1,0:T(8,128)S(1)} %gather_fusion.17, ...), kind=kOutput, calls=%fused_computation.199.clone.1 | convolution fusion | flops 318648320 | bytes 3801152 | tf_op jit(solution)/shard_map/while/body/eval_jaxpr/fga,fgb->gab/dot_general | solution.py:73
  293.3 8.8 %all-gather.6 = f32[1024,128]{1,0:T(8,128)S(1)} all-gather(f32[128,128]{1,0:T(8,128)S(1)} %get-tuple-element.795), channel_id=8, replica_groups=mesh['wide'=8,'narrow'=4] {'wide'}, dimensions={0}, use_global_device_ids=true | all-gather | bytes 589824 | tf_op jit(solution)/shard_map/all_gather | solution.py:17
  302.1 9.9 %all-gather.7 = f32[1024,128]{1,0:T(8,128)S(1)} all-gather(f32[128,128]{1,0:T(8,128)S(1)} %get-tuple-element.796), channel_id=9, replica_groups=mesh['wide'=8,'narrow'=4] {'wide'}, dimensions={0}, use_global_device_ids=true | all-gather | bytes 589824 | tf_op jit(solution)/shard_map/all_gather | solution.py:17
  (422 shorter events, 111.4 us)
Async XLA Ops:
  21.0 3.7 %copy-start.1 = (f32[50,16384]{1,0:T(8,128)S(1)}, f32[50,16384]{1,0:T(8,128)}, u32[]{:S(2)}) copy-start(f32[50,16384]{1,0:T(8,128)} %param.27) | copy-start | bytes 9830404
  24.7 0.9 copy-start.5
  24.7 2.1 copy-start.4
  27.0 70.9 %copy-start.3 = (f32[2048]{0:T(1024)S(1)}, f32[2048]{0:T(1024)}, u32[]{:S(2)}) copy-start(f32[2048]{0:T(1024)} %param.28) | copy-start | bytes 24580
  149.9 20.6 %copy-start.2 = (f32[16384]{0:T(1024)S(1)}, f32[16384]{0:T(1024)}, u32[]{:S(2)}) copy-start(f32[16384]{0:T(1024)} %param.29) | copy-start | bytes 196612
  293.2 20.0 %copy-start = (f32[16,128]{1,0:T(8,128)}, f32[16,128]{1,0:T(8,128)S(1)}, u32[]{:S(2)}) copy-start(f32[16,128]{1,0:T(8,128)S(1)} %get-tuple-element.2005) | copy-start | bytes 24580
where the time goes:
time: 314 us; the launch traced here: 313 us
  blocking collectives  109 us (35%)
  local copies, waits for them, and re-layouts  89.1 us (28%)
  matrix products  82 us (26%)
  other arithmetic  30 us (10%)
    all_gather x8, blocking collectives, combined_all(): everything = jax.tree.map(lambda part: lax.all_gather(part, axis), shard)  91.6 us
    dot_general x16, matrix products, cost_tiles(): jnp.einsum('fga,fgb->gab', source_part, target_part, precision=lax.Precis...  82 us
    gather x16, local copies, waits for them, and re-layouts, cost_tiles(): target_part = jnp.take(target_tiles, cols_of_slots, axis=1)  42.4 us
    all_gather x1, blocking collectives, local(): sources = lax.all_gather(source_features, 'narrow', axis=1, tiled=True)  17 us
    gather x16, local copies, waits for them, and re-layouts, cost_tiles(): source_part = jnp.take(source_tiles, rows_of_slots, axis=1)  9.73 us
    reduce_sum x16, other arithmetic, fold_into(): jnp.sum(jnp.where(belongs[:, :, None], masses[None] * jnp.exp(peaks[None]...  9.62 us
    gather x16, local copies, waits for them, and re-layouts, cost_tiles(): target_norm[cols_of_slots][:, None, :]  9.18 us
    gather x16, local copies, waits for them, and re-layouts, cost_tiles(): source_norm[rows_of_slots][:, :, None]  9.18 us

commit v1 on v0

v1 whole, which is shorter than its diff:
```python
import functools

import jax
import jax.numpy as jnp
from jax import lax
from jax.experimental import pallas as pl
from jax.experimental.pallas import tpu as pltpu
from jax.sharding import PartitionSpec as P

F = 50
TILE = 128
K_MAX = 8
ITERS = 2
PAD = 64

epsilon = 0.05
very_low = -1e30
product_scale = 2.0 / (F * epsilon)
norm_scale = 1.0 / (F * epsilon)


def split_three(x):
    first = x.astype(jnp.bfloat16)
    rest = x - first.astype(jnp.float32)
    second = rest.astype(jnp.bfloat16)
    third = (rest - second.astype(jnp.float32)).astype(jnp.bfloat16)
    return first, second, third


def padded(x):
    return jnp.concatenate([x, jnp.zeros((PAD - F, TILE), jnp.float32)], axis=0)


def kernel(
    wide_size,
    narrow_size,
    cols_ref,
    counts_ref,
    source_ref,
    target_ref,
    row_mass_ref,
    col_mass_ref,
    row_out_ref,
    col_out_ref,
    gathered,
    left,
    right,
    scores,
    one_hot,
    source_norm,
    target_norm,
    col_values,
    col_pieces,
    row_send,
    row_recv,
    slot_peak,
    slot_mass,
    col_peak,
    col_send,
    col_recv,
    gather_send_sem,
    gather_recv_sem,
    row_send_sem,
    row_recv_sem,
    scatter_send_sem,
    scatter_recv_sem,
    spread_send_sem,
    spread_recv_sem,
):
    wide = lax.axis_index("wide")
    narrow = lax.axis_index("narrow")
    row_count = cols_ref.shape[0]
    col_count = col_mass_ref.shape[0]
    shard_tiles = row_count // narrow_size
    piece = col_count // wide_size

    def wide_peer(d):
        return lax.rem(wide + d, wide_size)

    def narrow_peer(d):
        return lax.rem(narrow + d, narrow_size)

    def at_wide(w):
        return {"wide": w, "narrow": narrow}

    def at_narrow(z):
        return {"wide": wide, "narrow": z}

    def remote(src, dst, send, recv, where):
        return pltpu.make_async_remote_copy(
            src_ref=src,
            dst_ref=dst,
            send_sem=send,
            recv_sem=recv,
            device_id=where,
            device_id_type=pl.DeviceIdType.MESH,
        )

    barrier = pltpu.get_barrier_semaphore()
    for d in range(1, narrow_size):
        pl.semaphore_signal(
            barrier, inc=1, device_id=at_narrow(narrow_peer(d)), device_id_type=pl.DeviceIdType.MESH
        )
    for d in range(1, wide_size):
        pl.semaphore_signal(
            barrier, inc=1, device_id=at_wide(wide_peer(d)), device_id_type=pl.DeviceIdType.MESH
        )
    pl.semaphore_wait(barrier, narrow_size + wide_size - 2)

    def exchange(axis_size, peer, where, src_of, buffer, me, send_sem, recv_sem):
        sends = []
        for d in range(1, axis_size):
            to = peer(d)
            copy = remote(
                src_of(to), buffer.at[me], send_sem.at[d - 1], recv_sem.at[d - 1], where(to)
            )
            copy.start()
            sends.append(copy)

        def finish():
            for d in range(1, axis_size):
                origin = lax.rem(me + axis_size - d, axis_size)
                remote(
                    src_of(peer(d)),
                    buffer.at[origin],
                    send_sem.at[d - 1],
                    recv_sem.at[d - 1],
                    where(peer(d)),
                ).wait_recv()
            for copy in sends:
                copy.wait_send()

        return finish

    finish_gather = exchange(
        narrow_size,
        narrow_peer,
        at_narrow,
        lambda to: source_ref,
        gathered,
        narrow,
        gather_send_sem,
        gather_recv_sem,
    )
    gathered[narrow] = source_ref[...]

    def prepare_target(c, carry):
        x = padded(target_ref[:, pl.ds(pl.multiple_of(c * TILE, TILE), TILE)])
        first, second, third = split_three(x)
        right[c, 0:PAD, :] = first
        right[c, PAD : 2 * PAD, :] = second
        right[c, 2 * PAD : 3 * PAD, :] = third
        norm = jnp.sum(x * x, axis=0, keepdims=True) * norm_scale
        target_norm[pl.ds(c, 1), :] = norm
        return carry

    lax.fori_loop(0, col_count, prepare_target, 0)
    col_values[...] = -target_norm[...]
    finish_gather()

    lane = lax.broadcasted_iota(jnp.int32, (1, TILE), 1)

    def prepare_source(z, carry):
        for t in range(shard_tiles):
            r = z * shard_tiles + t
            x = padded(gathered[z, :, t * TILE : (t + 1) * TILE])
            source_norm[pl.ds(r, 1), :] = jnp.sum(x * x, axis=0, keepdims=True) * norm_scale
            first, second, third = split_three(x * product_scale)
            first, second, third = [p.astype(jnp.float32) for p in (first, second, third)]
            stacked = jnp.concatenate([first, first, first, second, second, third], axis=0)
            left[r] = jnp.transpose(stacked).astype(jnp.bfloat16)
        return carry

    lax.fori_loop(0, narrow_size, prepare_source, 0)

    def multiply(r, carry):
        a = left[r]
        marks = []
        for k in range(K_MAX):
            c = cols_ref[r, k]
            alive = k < counts_ref[r, 0]
            b = right[c]
            b = jnp.concatenate([b, b[0 : 2 * PAD], b[0:PAD]], axis=0)
            product = jnp.dot(a, b, preferred_element_type=jnp.float32)
            scores[r * K_MAX + k] = jnp.where(alive, product, very_low)
            marks.append((lane == jnp.where(alive, c, -1)).astype(jnp.float32))
        one_hot[pl.ds(pl.multiple_of(r * K_MAX, K_MAX), K_MAX), :] = jnp.concatenate(marks, axis=0)
        return carry

    lax.fori_loop(0, row_count, multiply, 0)

    half = TILE // 2
    row_lane = lax.broadcasted_iota(jnp.int32, (TILE, TILE), 1)

    def row_pass(step):
        def one_tile(r, carry):
            peaks, masses = carry
            tile_peaks, tile_masses = [], []
            values = [col_values[pl.ds(cols_ref[r, k], 1), :] for k in range(K_MAX)]
            for h in range(2):
                rows = slice(h * half, (h + 1) * half)
                top = None
                for k in range(K_MAX):
                    s = scores[r * K_MAX + k, rows, :] + values[k]
                    top = s if top is None else jnp.maximum(top, s)
                top = jnp.max(top, axis=1, keepdims=True)
                total = None
                for k in range(K_MAX):
                    s = jnp.exp(scores[r * K_MAX + k, rows, :] + values[k] - top)
                    total = s if total is None else total + s
                tile_peaks.append(top)
                tile_masses.append(jnp.sum(total, axis=1, keepdims=True))
            here = row_lane == r
            peaks = jnp.where(here, jnp.concatenate(tile_peaks, axis=0), peaks)
            masses = jnp.where(here, jnp.concatenate(tile_masses, axis=0), masses)
            return peaks, masses

        zero = jnp.zeros((TILE, TILE), jnp.float32)
        peaks, masses = lax.fori_loop(0, row_count, one_tile, (zero, zero))
        row_send[step, 0:row_count, :] = jnp.transpose(peaks)[0:row_count]
        row_send[step, row_count : 2 * row_count, :] = jnp.transpose(masses)[0:row_count]
        finish = exchange(
            narrow_size,
            narrow_peer,
            at_narrow,
            lambda to: row_send.at[step],
            row_recv.at[step],
            narrow,
            row_send_sem.at[step],
            row_recv_sem.at[step],
        )
        row_recv[step, narrow] = row_send[step]
        finish()
        parts = [row_recv[step, z] for z in range(narrow_size)]
        top = functools.reduce(jnp.maximum, [p[0:row_count] for p in parts])
        total = sum(p[row_count:] * jnp.exp(p[0:row_count] - top) for p in parts)
        return jnp.log(row_mass_ref[...]) - (top + jnp.log(total))

    col_index = lax.broadcasted_iota(jnp.int32, (col_count, TILE), 0)

    def col_pass(step, row_values_ref):
        def one_tile(r, highest):
            values = jnp.transpose(
                jnp.broadcast_to(row_values_ref[pl.ds(r, 1), :], (TILE, TILE))
            )
            peaks, masses = [], []
            for k in range(K_MAX):
                alive = k < counts_ref[r, 0]
                s = scores[r * K_MAX + k] + values
                top = jnp.max(s, axis=0, keepdims=True)
                total = jnp.sum(jnp.exp(s - top), axis=0, keepdims=True)
                top = jnp.where(alive, top, very_low)
                highest = jnp.where(
                    col_index == cols_ref[r, k], jnp.maximum(highest, top), highest
                )
                peaks.append(top)
                masses.append(jnp.where(alive, total, 0.0))
            place = pl.ds(pl.multiple_of(r * K_MAX, K_MAX), K_MAX)
            slot_peak[place, :] = jnp.concatenate(peaks, axis=0)
            slot_mass[place, :] = jnp.concatenate(masses, axis=0)
            return highest

        highest = lax.fori_loop(
            0, row_count, one_tile, jnp.full((col_count, TILE), very_low, jnp.float32)
        )
        col_peak[...] = highest

        def rescale(r, carry):
            place = pl.ds(pl.multiple_of(r * K_MAX, K_MAX), K_MAX)
            tops = jnp.concatenate(
                [col_peak[pl.ds(cols_ref[r, k], 1), :] for k in range(K_MAX)], axis=0
            )
            slot_mass[place, :] = slot_mass[place, :] * jnp.exp(
                jnp.minimum(slot_peak[place, :] - tops, 0.0)
            )
            return carry

        lax.fori_loop(0, row_count, rescale, 0)
        summed = lax.dot_general(
            one_hot[...],
            slot_mass[...],
            (((0,), (0,)), ((), ())),
            precision=lax.Precision.HIGHEST,
            preferred_element_type=jnp.float32,
        )
        for w in range(wide_size):
            col_send[step, w, 0] = highest[w * piece : (w + 1) * piece]
            col_send[step, w, 1] = summed[w * piece : (w + 1) * piece]
        finish = exchange(
            wide_size,
            wide_peer,
            at_wide,
            lambda to: col_send.at[step, to],
            col_recv.at[step],
            wide,
            scatter_send_sem.at[step],
            scatter_recv_sem.at[step],
        )
        col_recv[step, wide] = col_send[step, wide]
        finish()
        parts = [col_recv[step, w] for w in range(wide_size)]
        top = functools.reduce(jnp.maximum, [p[0] for p in parts])
        total = sum(p[1] * jnp.exp(p[0] - top) for p in parts)
        mass = col_mass_ref[pl.ds(pl.multiple_of(wide * piece, piece), piece), :]
        col_pieces[step, wide] = jnp.log(mass) - (top + jnp.log(total))
        finish = exchange(
            wide_size,
            wide_peer,
            at_wide,
            lambda to: col_pieces.at[step, wide],
            col_pieces.at[step],
            wide,
            spread_send_sem.at[step],
            spread_recv_sem.at[step],
        )
        finish()
        for w in range(wide_size):
            col_values[w * piece : (w + 1) * piece, :] = col_pieces[step, w]

    for step in range(ITERS):
        row_out_ref[...] = row_pass(step)
        col_pass(step, row_out_ref)
    row_out_ref[...] = epsilon * (row_out_ref[...] + source_norm[...])
    col_out_ref[...] = epsilon * (col_values[...] + target_norm[...])


def local(
    wide_size,
    narrow_size,
    source_features,
    target_features,
    source_mass,
    target_mass,
    block_cols,
    block_counts,
):
    row_count = source_mass.shape[0] // TILE
    col_count = target_mass.shape[0] // TILE
    slots = row_count * K_MAX
    piece = col_count // wide_size
    vmem = pl.BlockSpec(memory_space=pltpu.VMEM)
    smem = pl.BlockSpec(memory_space=pltpu.SMEM)
    f32 = jnp.float32
    dma = pltpu.SemaphoreType.DMA
    rows, cols = pl.pallas_call(
        functools.partial(kernel, wide_size, narrow_size),
        out_shape=(
            jax.ShapeDtypeStruct((row_count, TILE), f32),
            jax.ShapeDtypeStruct((col_count, TILE), f32),
        ),
        in_specs=[smem, smem, vmem, vmem, vmem, vmem],
        out_specs=(vmem, vmem),
        scratch_shapes=[
            pltpu.VMEM((narrow_size, F, source_features.shape[1]), f32),
            pltpu.VMEM((row_count, TILE, 6 * PAD), jnp.bfloat16),
            pltpu.VMEM((col_count, 3 * PAD, TILE), jnp.bfloat16),
            pltpu.VMEM((slots, TILE, TILE), f32),
            pltpu.VMEM((slots, col_count), f32),
            pltpu.VMEM((row_count, TILE), f32),
            pltpu.VMEM((col_count, TILE), f32),
            pltpu.VMEM((col_count, TILE), f32),
            pltpu.VMEM((ITERS, wide_size, piece, TILE), f32),
            pltpu.VMEM((ITERS, 2 * row_count, TILE), f32),
            pltpu.VMEM((ITERS, narrow_size, 2 * row_count, TILE), f32),
            pltpu.VMEM((slots, TILE), f32),
            pltpu.VMEM((slots, TILE), f32),
            pltpu.VMEM((col_count, TILE), f32),
            pltpu.VMEM((ITERS, wide_size, 2, piece, TILE), f32),
            pltpu.VMEM((ITERS, wide_size, 2, piece, TILE), f32),
            dma((narrow_size - 1,)),
            dma((narrow_size - 1,)),
            dma((ITERS, narrow_size - 1)),
            dma((ITERS, narrow_size - 1)),
            dma((ITERS, wide_size - 1)),
            dma((ITERS, wide_size - 1)),
            dma((ITERS, wide_size - 1)),
            dma((ITERS, wide_size - 1)),
        ],
        compiler_params=pltpu.CompilerParams(
            collective_id=0, has_side_effects=True, vmem_limit_bytes=50 << 20
        ),
    )(
        block_cols,
        block_counts,
        source_features,
        target_features,
        source_mass.reshape(row_count, TILE),
        target_mass.reshape(col_count, TILE),
    )
    return rows.reshape(-1), cols.reshape(-1)


def solution(mesh):
    in_specs = (
        P(None, ("wide", "narrow")),
        P(None, "narrow"),
        P("wide"),
        P("narrow"),
        P("wide", "narrow"),
        P("wide", "narrow"),
    )
    out_specs = (P("wide"), P("narrow"))
    return jax.shard_map(
        functools.partial(local, mesh.shape["wide"], mesh.shape["narrow"]),
        mesh=mesh,
        in_specs=in_specs,
        out_specs=out_specs,
        check_vma=False,
    )
```

time: 314 us -> 75.4 us (0.24)
  blocking collectives: 109 us -> 0 us
  matrix products: 82 us -> 0 us
  local copies, waits for them, and re-layouts: 89.1 us -> 7.2 us
  Pallas kernels: 0 us -> 67.2 us
  other arithmetic: 30 us -> 0 us
    all_gather x9 -> x0, blocking collectives: 109 us -> none  [the longest x8 91.6 us: combined_all(): everything = jax.tree.map(lambda part: lax.all_gather(part, axis), shard)]
    dot_general x16 -> x0, matrix products: 82 us -> none  [cost_tiles(): jnp.einsum('fga,fgb->gab', source_part, target_part, precision=lax.Precis...]
    gather x80 -> x0, local copies, waits for them, and re-layouts: 79.6 us -> none  [the longest x16 42.4 us: cost_tiles(): target_part = jnp.take(target_tiles, cols_of_slots, axis=1)]
    pallas_call x0 -> x1, Pallas kernels: none -> 67.2 us  [local(): pl.pallas_call(functools.partial(kernel, wide_size, narrow_size), out_sha...]
    reduce_sum x34 -> x0, other arithmetic: 15.6 us -> none  [the longest x16 9.62 us: fold_into(): jnp.sum(jnp.where(belongs[:, :, None], masses[None] * jnp.exp(peaks[None]...]
    reduce_max x16 -> x0, other arithmetic: 8.76 us -> none  [fold_into(): jnp.max(jnp.where(belongs[:, :, None], peaks[None], very_low), axis=1)]
    unnamed x18 -> x12, local copies, waits for them, and re-layouts: 7.22 us -> 7.2 us
where the time goes in v1:
time: 75.4 us; the launch traced here: 75.1 us
  Pallas kernels  67.2 us (89%)
  local copies, waits for them, and re-layouts  7.2 us (10%)
    pallas_call x1, Pallas kernels, local(): pl.pallas_call(functools.partial(kernel, wide_size, narrow_size), out_sha...  67.2 us
    unnamed x12, local copies, waits for them, and re-layouts  7.2 us

profile of v1, /device:TPU:0, one launch (start us, length us, event | category | flops | bytes accessed | tf_op | source)
XLA Modules:
  0.0 75.1 jit_solution(6643490482723855335)
XLA Ops:
  0.6 0.8 %copy.8.cols_ref = s32[16,8]{1,0:T(8,128)S(1)} copy(s32[16,8]{0,1:T(8,128)} %param.10) | data formatting | bytes 1024 | tf_op args[4]
  1.4 0.7 copy.9.counts_ref
  2.1 0.0 copy-start
  2.1 2.0 %copy-done = f32[50,16384]{1,0:T(8,128)S(1)} copy-done((f32[50,16384]{1,0:T(8,128)S(1)}, f32[50,16384]{1,0:T(8,128)}, u32[]{:S(2)}) %copy-start) | copy-done | bytes 3276824
  4.2 0.0 copy-start.1
  4.2 0.9 %copy-done.1 = f32[50,512]{1,0:T(8,128)S(1)} copy-done((f32[50,512]{1,0:T(8,128)S(1)}, f32[50,512]{1,0:T(8,128)}, u32[]{:S(2)}) %copy-start.1) | copy-done | bytes 102424
  5.1 0.0 copy-start.2
  5.1 0.8 %copy-done.2 = f32[16384]{0:T(1024)S(1)} copy-done((f32[16384]{0:T(1024)S(1)}, f32[16384]{0:T(1024)}, u32[]{:S(2)}) %copy-start.2) | copy-done | bytes 65560
  5.9 0.0 copy-start.3
  5.9 0.7 copy-done.3
  6.6 67.2 %shard_map.77 = (f32[16,128]{1,0:T(8,128)S(1)}, f32[128,128]{1,0:T(8,128)S(1)}) custom-call(s32[16,8]{1,0:T(8,128)S(1)} %copy.8.cols_ref, s32[16,1]{1,0:T(8,128)S(1)} %copy.9.counts_ref, f32[50,512]{1,0:T(8,128)S(1)} %copy-done.1, f32[50,16384]{1,0:T(8,128)S(1)} %copy-done, f32[16,128]{1,0:T(8,128)S(1)} %bitcast.6, f32[128,128]{1,0:T(8,128)S(1)} %bitcast.4), custom_call_target="tpu_custom_call" | custom-call | tf_op jit(solution)/shard_map/pallas_call | solution.py:345
  73.8 0.6 copy.12
  74.4 0.6 copy.13
Async XLA Ops:
  2.1 2.0 %copy-start = (f32[50,16384]{1,0:T(8,128)S(1)}, f32[50,16384]{1,0:T(8,128)}, u32[]{:S(2)}) copy-start(f32[50,16384]{1,0:T(8,128)} %target_ref.1) | copy-start | bytes 9830404
  4.2 0.9 %copy-start.1 = (f32[50,512]{1,0:T(8,128)S(1)}, f32[50,512]{1,0:T(8,128)}, u32[]{:S(2)}) copy-start(f32[50,512]{1,0:T(8,128)} %source_ref.1) | copy-start | bytes 307204
  5.1 0.8 %copy-start.2 = (f32[16384]{0:T(1024)S(1)}, f32[16384]{0:T(1024)}, u32[]{:S(2)}) copy-start(f32[16384]{0:T(1024)} %param.9) | copy-start | bytes 196612
  5.9 0.7 copy-start.3

commit v2 on v1

v2 whole, which is shorter than its diff:
```python
import functools

import jax
import jax.numpy as jnp
from jax import lax
from jax.experimental import pallas as pl
from jax.experimental.pallas import tpu as pltpu
from jax.sharding import PartitionSpec as P

F = 50
TILE = 128
K_MAX = 8
ITERS = 2
PAD = 64
CHUNKS = 4

epsilon = 0.05
very_low = -1e30
log2_e = 1.4426950408889634
product_scale = 2.0 * log2_e / (F * epsilon)
norm_scale = log2_e / (F * epsilon)
potential_scale = epsilon / log2_e


def split_three(x):
    first = x.astype(jnp.bfloat16)
    rest = x - first.astype(jnp.float32)
    second = rest.astype(jnp.bfloat16)
    third = (rest - second.astype(jnp.float32)).astype(jnp.bfloat16)
    return first, second, third


def log2(x):
    return jnp.log(x) * log2_e


def padded(x):
    return jnp.concatenate([x, jnp.zeros((PAD - F, TILE), jnp.float32)], axis=0)


def kernel(
    wide_size,
    narrow_size,
    cols_ref,
    counts_ref,
    source_hbm,
    target_hbm,
    row_mass_hbm,
    col_mass_hbm,
    row_out_ref,
    col_out_ref,
    gathered,
    target_ref,
    row_mass_ref,
    col_mass_ref,
    right,
    scores,
    one_hot,
    marked,
    source_norm,
    target_norm,
    col_values,
    col_pieces,
    row_columns,
    row_send,
    row_recv,
    slot_lse,
    slot_mass,
    col_peak,
    col_send,
    col_recv,
    load_sem,
    gather_send_sem,
    gather_recv_sem,
    row_send_sem,
    row_recv_sem,
    scatter_send_sem,
    scatter_recv_sem,
    spread_send_sem,
    spread_recv_sem,
):
    wide = lax.axis_index("wide")
    narrow = lax.axis_index("narrow")
    row_count = row_mass_ref.shape[0]
    col_count = col_mass_ref.shape[0]
    shard_tiles = row_count // narrow_size
    piece = col_count // wide_size
    chunk_tiles = col_count // CHUNKS
    chunk_cols = chunk_tiles * TILE

    def wide_peer(d):
        return lax.rem(wide + d, wide_size)

    def narrow_peer(d):
        return lax.rem(narrow + d, narrow_size)

    def at_wide(w):
        return {"wide": w, "narrow": narrow}

    def at_narrow(z):
        return {"wide": wide, "narrow": z}

    def remote(src, dst, send, recv, where):
        return pltpu.make_async_remote_copy(
            src_ref=src,
            dst_ref=dst,
            send_sem=send,
            recv_sem=recv,
            device_id=where,
            device_id_type=pl.DeviceIdType.MESH,
        )

    barrier = pltpu.get_barrier_semaphore()
    for d in range(1, narrow_size):
        pl.semaphore_signal(
            barrier, inc=1, device_id=at_narrow(narrow_peer(d)), device_id_type=pl.DeviceIdType.MESH
        )
    for d in range(1, wide_size):
        pl.semaphore_signal(
            barrier, inc=1, device_id=at_wide(wide_peer(d)), device_id_type=pl.DeviceIdType.MESH
        )
    loads = [pltpu.make_async_copy(source_hbm, gathered.at[narrow], load_sem.at[CHUNKS])]
    for q in range(CHUNKS):
        part = pl.ds(q * chunk_cols, chunk_cols)
        loads.append(
            pltpu.make_async_copy(target_hbm.at[:, part], target_ref.at[:, part], load_sem.at[q])
        )
    loads.append(pltpu.make_async_copy(row_mass_hbm, row_mass_ref, load_sem.at[CHUNKS + 1]))
    loads.append(pltpu.make_async_copy(col_mass_hbm, col_mass_ref, load_sem.at[CHUNKS + 2]))
    for load in loads:
        load.start()
    pl.semaphore_wait(barrier, narrow_size + wide_size - 2)

    def exchange(axis_size, peer, where, src_of, buffer, me, send_sem, recv_sem):
        sends = []
        for d in range(1, axis_size):
            to = peer(d)
            copy = remote(
                src_of(to), buffer.at[me], send_sem.at[d - 1], recv_sem.at[d - 1], where(to)
            )
            copy.start()
            sends.append(copy)

        def arrive(d):
            origin = lax.rem(me + axis_size - d, axis_size)
            remote(
                src_of(peer(d)),
                buffer.at[origin],
                send_sem.at[d - 1],
                recv_sem.at[d - 1],
                where(peer(d)),
            ).wait_recv()

        def leave():
            for copy in sends:
                copy.wait_send()

        def finish():
            for d in range(1, axis_size):
                arrive(d)
            leave()

        return finish, arrive, leave

    _, gather_arrive, gather_leave = exchange(
        narrow_size,
        narrow_peer,
        at_narrow,
        lambda to: source_hbm,
        gathered,
        narrow,
        gather_send_sem,
        gather_recv_sem,
    )

    def prepare_target(c, carry):
        x = padded(target_ref[:, pl.ds(pl.multiple_of(c * TILE, TILE), TILE)])
        first, second, third = split_three(x)
        right[c, 0:PAD, :] = first
        right[c, PAD : 2 * PAD, :] = second
        right[c, 2 * PAD : 3 * PAD, :] = third
        norm = jnp.sum(x * x, axis=0, keepdims=True) * norm_scale
        target_norm[pl.ds(c, 1), :] = norm
        return carry

    loads[0].wait()
    for q in range(CHUNKS):
        loads[q + 1].wait()
        lax.fori_loop(q * chunk_tiles, (q + 1) * chunk_tiles, prepare_target, 0)
    col_values[...] = -target_norm[...]
    loads[CHUNKS + 1].wait()
    loads[CHUNKS + 2].wait()

    lane = lax.broadcasted_iota(jnp.int32, (1, TILE), 1)
    row_lane = lax.broadcasted_iota(jnp.int32, (TILE, TILE), 1)
    slab = 8

    def row_tile(r):
        values = [col_values[pl.ds(cols_ref[k, r], 1), :] for k in range(K_MAX)]
        tops, totals = [], []
        for h in range(TILE // slab):
            rows = slice(h * slab, (h + 1) * slab)
            s = [scores[r * K_MAX + k, rows, :] + values[k] for k in range(K_MAX)]
            top = functools.reduce(jnp.maximum, s)
            totals.append(sum(jnp.exp2(x - top) for x in s))
            tops.append(top)
        top = jnp.concatenate(tops, axis=0)
        total = jnp.concatenate(totals, axis=0)
        peak = jnp.max(top, axis=1, keepdims=True)
        mass = jnp.sum(total * jnp.exp2(top - peak), axis=1, keepdims=True)
        row_columns[...] = jnp.where(
            row_lane == r,
            peak,
            jnp.where(row_lane == r + TILE // 2, mass, row_columns[...]),
        )

    def first_tile(r, x):
        source_norm[pl.ds(r, 1), :] = jnp.sum(x * x, axis=0, keepdims=True) * norm_scale
        first, second, third = split_three(x * product_scale)
        first, second, third = [p.astype(jnp.float32) for p in (first, second, third)]
        stacked = jnp.concatenate([first, first, first, second, second, third], axis=0)
        a = jnp.transpose(stacked).astype(jnp.bfloat16)
        marks = []
        for k in range(0, K_MAX, 2):
            pair = []
            for j in (k, k + 1):
                c = cols_ref[j, r]
                alive = j < counts_ref[0, r]
                b = right[c]
                pair.append(jnp.concatenate([b, b[0 : 2 * PAD], b[0:PAD]], axis=0))
                marks.append((lane == jnp.where(alive, c, -1)).astype(jnp.float32))
            product = jnp.dot(
                a, jnp.concatenate(pair, axis=1), preferred_element_type=jnp.float32
            )
            for j in (k, k + 1):
                alive = j < counts_ref[0, r]
                part = product[:, (j - k) * TILE : (j - k + 1) * TILE]
                scores[r * K_MAX + j] = jnp.where(alive, part, very_low)
        marks = jnp.concatenate(marks, axis=0)
        one_hot[pl.ds(pl.multiple_of(r * K_MAX, K_MAX), K_MAX), :] = marks
        unmarked = 1.0 - jnp.sum(marks, axis=0, keepdims=True)
        marked[r] = jnp.concatenate(
            [marks, marks, unmarked, jnp.zeros((2 * K_MAX - 1, TILE), jnp.float32)], axis=0
        ).astype(jnp.bfloat16)
        row_tile(r)

    row_columns[...] = jnp.zeros((TILE, TILE), jnp.float32)
    for d in range(narrow_size):
        if d > 0:
            gather_arrive(d)
        z = lax.rem(narrow + narrow_size - d, narrow_size)

        def one(t, carry):
            x = padded(gathered[z, :, pl.ds(pl.multiple_of(t * TILE, TILE), TILE)])
            first_tile(z * shard_tiles + t, x)
            return carry

        lax.fori_loop(0, shard_tiles, one, 0)
    gather_leave()

    def row_combine(step):
        columns = jnp.transpose(row_columns[...])
        half = TILE // 2
        row_send[step] = columns[0:row_count] + log2(columns[half : half + row_count])
        finish, _, _ = exchange(
            narrow_size,
            narrow_peer,
            at_narrow,
            lambda to: row_send.at[step],
            row_recv.at[step],
            narrow,
            row_send_sem.at[step],
            row_recv_sem.at[step],
        )
        row_recv[step, narrow] = row_send[step]
        finish()
        parts = [row_recv[step, z] for z in range(narrow_size)]
        top = functools.reduce(jnp.maximum, parts)
        total = sum(jnp.exp2(p - top) for p in parts)
        return log2(row_mass_ref[...]) - (top + log2(total))

    def col_pass(step, row_values_ref):
        def one_tile(r, carry):
            values = jnp.transpose(
                jnp.broadcast_to(row_values_ref[pl.ds(r, 1), :], (TILE, TILE))
            )
            results = []
            for k in range(K_MAX):
                s = [
                    scores[r * K_MAX + k, h * slab : (h + 1) * slab, :]
                    + values[h * slab : (h + 1) * slab]
                    for h in range(TILE // slab)
                ]
                top = functools.reduce(jnp.maximum, s)
                total = sum(jnp.exp2(x - top) for x in s)
                peak = jnp.max(top, axis=0, keepdims=True)
                mass = jnp.sum(total * jnp.exp2(top - peak), axis=0, keepdims=True)
                alive = k < counts_ref[0, r]
                results.append((jnp.where(alive, peak, very_low), mass))
            lse = jnp.concatenate([p for p, _ in results], axis=0) + log2(
                jnp.concatenate([m for _, m in results], axis=0)
            )
            slot_lse[pl.ds(pl.multiple_of(r * K_MAX, K_MAX), K_MAX), :] = lse
            coarse = lse.astype(jnp.bfloat16).astype(jnp.float32)
            stack = jnp.concatenate(
                [
                    coarse,
                    lse - coarse,
                    jnp.full((1, TILE), very_low, jnp.float32),
                    jnp.zeros((2 * K_MAX - 1, TILE), jnp.float32),
                ],
                axis=0,
            ).astype(jnp.bfloat16)
            spread = lax.dot_general(
                marked[r],
                stack,
                (((0,), (0,)), ((), ())),
                preferred_element_type=jnp.float32,
            )
            col_peak[...] = jnp.maximum(col_peak[...], spread)
            return carry

        col_peak[...] = jnp.full((col_count, TILE), very_low, jnp.float32)
        lax.fori_loop(0, row_count, one_tile, 0)

        def rescale(r, carry):
            place = pl.ds(pl.multiple_of(r * K_MAX, K_MAX), K_MAX)
            tops = jnp.concatenate(
                [col_peak[pl.ds(cols_ref[k, r], 1), :] for k in range(K_MAX)], axis=0
            )
            slot_mass[place, :] = jnp.exp2(jnp.minimum(slot_lse[place, :] - tops, 1e2))
            return carry

        lax.fori_loop(0, row_count, rescale, 0)
        summed = lax.dot_general(
            one_hot[...],
            slot_mass[...],
            (((0,), (0,)), ((), ())),
            precision=lax.Precision.HIGHEST,
            preferred_element_type=jnp.float32,
        )
        lse = jnp.where(
            summed > 0.0, col_peak[...] + log2(jnp.maximum(summed, 1e-30)), very_low
        )
        for w in range(wide_size):
            col_send[step, w] = lse[w * piece : (w + 1) * piece]
        finish, _, _ = exchange(
            wide_size,
            wide_peer,
            at_wide,
            lambda to: col_send.at[step, to],
            col_recv.at[step],
            wide,
            scatter_send_sem.at[step],
            scatter_recv_sem.at[step],
        )
        col_recv[step, wide] = col_send[step, wide]
        finish()
        parts = [col_recv[step, w] for w in range(wide_size)]
        top = functools.reduce(jnp.maximum, parts)
        total = sum(jnp.exp2(p - top) for p in parts)
        mass = col_mass_ref[pl.ds(pl.multiple_of(wide * piece, piece), piece), :]
        col_pieces[step, wide] = log2(mass) - (top + log2(total))
        finish, _, _ = exchange(
            wide_size,
            wide_peer,
            at_wide,
            lambda to: col_pieces.at[step, wide],
            col_pieces.at[step],
            wide,
            spread_send_sem.at[step],
            spread_recv_sem.at[step],
        )
        finish()
        for w in range(wide_size):
            col_values[w * piece : (w + 1) * piece, :] = col_pieces[step, w]

    def row_pass(r, carry):
        row_tile(r)
        return carry

    for step in range(ITERS):
        if step > 0:
            lax.fori_loop(0, row_count, row_pass, 0)
        row_out_ref[...] = row_combine(step)
        col_pass(step, row_out_ref)
    row_out_ref[...] = potential_scale * (row_out_ref[...] + source_norm[...])
    col_out_ref[...] = potential_scale * (col_values[...] + target_norm[...])


def local(
    wide_size,
    narrow_size,
    source_features,
    target_features,
    source_mass,
    target_mass,
    block_cols,
    block_counts,
):
    row_count = source_mass.shape[0] // TILE
    col_count = target_mass.shape[0] // TILE
    slots = row_count * K_MAX
    piece = col_count // wide_size
    vmem = pl.BlockSpec(memory_space=pltpu.VMEM)
    smem = pl.BlockSpec(memory_space=pltpu.SMEM)
    hbm = pl.BlockSpec(memory_space=pltpu.HBM)
    f32 = jnp.float32
    dma = pltpu.SemaphoreType.DMA
    rows, cols = pl.pallas_call(
        functools.partial(kernel, wide_size, narrow_size),
        out_shape=(
            jax.ShapeDtypeStruct((row_count, TILE), f32),
            jax.ShapeDtypeStruct((col_count, TILE), f32),
        ),
        in_specs=[smem, smem, hbm, hbm, hbm, hbm],
        out_specs=(vmem, vmem),
        scratch_shapes=[
            pltpu.VMEM((narrow_size, F, source_features.shape[1]), f32),
            pltpu.VMEM(target_features.shape, f32),
            pltpu.VMEM((row_count, TILE), f32),
            pltpu.VMEM((col_count, TILE), f32),
            pltpu.VMEM((col_count, 3 * PAD, TILE), jnp.bfloat16),
            pltpu.VMEM((slots, TILE, TILE), f32),
            pltpu.VMEM((slots, col_count), f32),
            pltpu.VMEM((row_count, 4 * K_MAX, col_count), jnp.bfloat16),
            pltpu.VMEM((row_count, TILE), f32),
            pltpu.VMEM((col_count, TILE), f32),
            pltpu.VMEM((col_count, TILE), f32),
            pltpu.VMEM((ITERS, wide_size, piece, TILE), f32),
            pltpu.VMEM((TILE, TILE), f32),
            pltpu.VMEM((ITERS, row_count, TILE), f32),
            pltpu.VMEM((ITERS, narrow_size, row_count, TILE), f32),
            pltpu.VMEM((slots, TILE), f32),
            pltpu.VMEM((slots, TILE), f32),
            pltpu.VMEM((col_count, TILE), f32),
            pltpu.VMEM((ITERS, wide_size, piece, TILE), f32),
            pltpu.VMEM((ITERS, wide_size, piece, TILE), f32),
            dma((CHUNKS + 3,)),
            dma((narrow_size - 1,)),
            dma((narrow_size - 1,)),
            dma((ITERS, narrow_size - 1)),
            dma((ITERS, narrow_size - 1)),
            dma((ITERS, wide_size - 1)),
            dma((ITERS, wide_size - 1)),
            dma((ITERS, wide_size - 1)),
            dma((ITERS, wide_size - 1)),
        ],
        compiler_params=pltpu.CompilerParams(
            collective_id=0, has_side_effects=True, vmem_limit_bytes=67043328
        ),
    )(
        block_cols.T,
        block_counts.T,
        source_features,
        target_features,
        source_mass.reshape(row_count, TILE),
        target_mass.reshape(col_count, TILE),
    )
    return rows.reshape(-1), cols.reshape(-1)


def solution(mesh):
    in_specs = (
        P(None, ("wide", "narrow")),
        P(None, "narrow"),
        P("wide"),
        P("narrow"),
        P("wide", "narrow"),
        P("wide", "narrow"),
    )
    out_specs = (P("wide"), P("narrow"))
    return jax.shard_map(
        functools.partial(local, mesh.shape["wide"], mesh.shape["narrow"]),
        mesh=mesh,
        in_specs=in_specs,
        out_specs=out_specs,
        check_vma=False,
    )
```

time: 75.4 us -> 61.5 us (0.82)
  Pallas kernels: 67.2 us -> 57.9 us
  local copies, waits for them, and re-layouts: 7.2 us -> 2.77 us
    pallas_call x1, Pallas kernels: 67.2 us -> 57.9 us  [local(): pl.pallas_call(functools.partial(kernel, wide_size, narrow_size), out_sha...]
    unnamed x12 -> x2, local copies, waits for them, and re-layouts: 7.2 us -> 2.77 us
where the time goes in v2:
time: 61.5 us; the launch traced here: 61.3 us
  Pallas kernels  57.9 us (94%)
  local copies, waits for them, and re-layouts  2.77 us (5%)
  between operations  0.64 us (1%)
    pallas_call x1, Pallas kernels, local(): pl.pallas_call(functools.partial(kernel, wide_size, narrow_size), out_sha...  57.9 us
    unnamed x2, local copies, waits for them, and re-layouts  2.77 us

profile of v2, /device:TPU:0, one launch (start us, length us, event | category | flops | bytes accessed | tf_op | source)
XLA Modules:
  0.0 61.3 jit_solution(2614918302944137613)
XLA Ops:
  0.6 57.9 %shard_map.77 = (f32[16,128]{1,0:T(8,128)}, f32[128,128]{1,0:T(8,128)}) custom-call(s32[8,16]{1,0:T(8,128)} %bitcast.10, s32[1,16]{1,0:T(1,128)} %bitcast.11, f32[50,512]{1,0:T(8,128)} %source_hbm.1, f32[50,16384]{1,0:T(8,128)} %target_hbm.1, f32[16,128]{1,0:T(8,128)} %bitcast.8, f32[128,128]{1,0:T(8,128)} %bitcast.6), custom_call_target="tpu_custom_call" | custom-call | tf_op jit(solution)/shard_map/pallas_call | solution.py:410
  58.5 1.3 %copy.10 = f32[2048]{0:T(1024)} copy(f32[2048]{0:T(1024)} %bitcast.9) | data formatting | bytes 16384
  59.8 1.5 %copy.11 = f32[16384]{0:T(1024)} copy(f32[16384]{0:T(1024)} %bitcast.7) | data formatting | bytes 131072

commit v3 on v2

--- a/solution.py
+++ b/solution.py
@@ -13,6 +13,8 @@
 ITERS = 2
 PAD = 64
 CHUNKS = 4
+SLABS = 16
+GROUP = 4
 
 epsilon = 0.05
 very_low = -1e30
@@ -32,6 +34,22 @@
 
 def log2(x):
     return jnp.log(x) * log2_e
+
+
+def paired(me, d, size):
+    other, bit = 0, 1
+    while bit < size:
+        other = other + lax.rem(lax.div(me, bit) + d // bit % 2, 2) * bit
+        bit *= 2
+    return other
+
+
+def tree(combine, parts):
+    parts = list(parts)
+    while len(parts) > 1:
+        pairs = [combine(a, b) for a, b in zip(parts[0::2], parts[1::2])]
+        parts = pairs + parts[len(parts) // 2 * 2 :]
+    return parts[0]
 
 
 def padded(x):
@@ -61,7 +79,8 @@
     target_norm,
     col_values,
     col_pieces,
-    row_columns,
+    lane_peak,
+    lane_mass,
     row_send,
     row_recv,
     slot_lse,
@@ -89,10 +108,10 @@
     chunk_cols = chunk_tiles * TILE
 
     def wide_peer(d):
-        return lax.rem(wide + d, wide_size)
+        return paired(wide, d, wide_size)
 
     def narrow_peer(d):
-        return lax.rem(narrow + d, narrow_size)
+        return paired(narrow, d, narrow_size)
 
     def at_wide(w):
         return {"wide": w, "narrow": narrow}
@@ -142,10 +161,9 @@
             sends.append(copy)
 
         def arrive(d):
-            origin = lax.rem(me + axis_size - d, axis_size)
             remote(
                 src_of(peer(d)),
-                buffer.at[origin],
+                buffer.at[peer(d)],
                 send_sem.at[d - 1],
                 recv_sem.at[d - 1],
                 where(peer(d)),
@@ -196,23 +214,37 @@
     slab = 8
 
     def row_tile(r):
-        values = [col_values[pl.ds(cols_ref[k, r], 1), :] for k in range(K_MAX)]
-        tops, totals = [], []
-        for h in range(TILE // slab):
-            rows = slice(h * slab, (h + 1) * slab)
-            s = [scores[r * K_MAX + k, rows, :] + values[k] for k in range(K_MAX)]
-            top = functools.reduce(jnp.maximum, s)
-            totals.append(sum(jnp.exp2(x - top) for x in s))
-            tops.append(top)
-        top = jnp.concatenate(tops, axis=0)
-        total = jnp.concatenate(totals, axis=0)
-        peak = jnp.max(top, axis=1, keepdims=True)
-        mass = jnp.sum(total * jnp.exp2(top - peak), axis=1, keepdims=True)
-        row_columns[...] = jnp.where(
-            row_lane == r,
-            peak,
-            jnp.where(row_lane == r + TILE // 2, mass, row_columns[...]),
-        )
+        values = [
+            jnp.broadcast_to(col_values[pl.ds(cols_ref[k, r], 1), :], (slab, TILE))
+            for k in range(K_MAX)
+        ]
+
+        def one_group(g, carry):
+            for h in range(SLABS):
+                rows = pl.ds(pl.multiple_of((g * SLABS + h) * slab, slab), slab)
+                s = [scores[r * K_MAX + k, rows, :] + values[k] for k in range(K_MAX)]
+                top = tree(jnp.maximum, s)
+                lane_mass[r, rows, :] = tree(jnp.add, [jnp.exp2(x - top) for x in s])
+                lane_peak[r, rows, :] = top
+            return carry
+
+        lax.fori_loop(0, TILE // (slab * SLABS), one_group, 0)
+
+    def row_reduce():
+        def one_group(g, columns):
+            for j in range(GROUP):
+                r = g * GROUP + j
+                top = lane_peak[r]
+                peak = jnp.max(top, axis=1, keepdims=True)
+                mass = jnp.sum(lane_mass[r] * jnp.exp2(top - peak), axis=1, keepdims=True)
+                columns = jnp.where(row_lane == r, peak, columns)
+                columns = jnp.where(row_lane == r + TILE // 2, mass, columns)
+            return columns
+
+        columns = lax.fori_loop(
+            0, row_count // GROUP, one_group, jnp.zeros((TILE, TILE), jnp.float32)
+        )
+        return jnp.transpose(columns)
 
     def first_tile(r, x):
         source_norm[pl.ds(r, 1), :] = jnp.sum(x * x, axis=0, keepdims=True) * norm_scale
@@ -244,11 +276,10 @@
         ).astype(jnp.bfloat16)
         row_tile(r)
 
-    row_columns[...] = jnp.zeros((TILE, TILE), jnp.float32)
     for d in range(narrow_size):
         if d > 0:
             gather_arrive(d)
-        z = lax.rem(narrow + narrow_size - d, narrow_size)
+        z = narrow_peer(d)
 
         def one(t, carry):
             x = padded(gathered[z, :, pl.ds(pl.multiple_of(t * TILE, TILE), TILE)])
@@ -259,7 +290,7 @@
     gather_leave()
 
     def row_combine(step):
-        columns = jnp.transpose(row_columns[...])
+        columns = row_reduce()
         half = TILE // 2
         row_send[step] = columns[0:row_count] + log2(columns[half : half + row_count])
         finish, _, _ = exchange(
@@ -291,8 +322,8 @@
                     + values[h * slab : (h + 1) * slab]
                     for h in range(TILE // slab)
                 ]
-                top = functools.reduce(jnp.maximum, s)
-                total = sum(jnp.exp2(x - top) for x in s)
+                top = tree(jnp.maximum, s)
+                total = tree(jnp.add, [jnp.exp2(x - top) for x in s])
                 peak = jnp.max(top, axis=0, keepdims=True)
                 mass = jnp.sum(total * jnp.exp2(top - peak), axis=0, keepdims=True)
                 alive = k < counts_ref[0, r]
@@ -428,7 +459,8 @@
             pltpu.VMEM((col_count, TILE), f32),
             pltpu.VMEM((col_count, TILE), f32),
             pltpu.VMEM((ITERS, wide_size, piece, TILE), f32),
-            pltpu.VMEM((TILE, TILE), f32),
+            pltpu.VMEM((row_count, TILE, TILE), f32),
+            pltpu.VMEM((row_count, TILE, TILE), f32),
             pltpu.VMEM((ITERS, row_count, TILE), f32),
             pltpu.VMEM((ITERS, narrow_size, row_count, TILE), f32),
             pltpu.VMEM((slots, TILE), f32),

time: 61.5 us -> 60.3 us (0.980)
  Pallas kernels: 57.9 us -> 56.7 us
    pallas_call x1, Pallas kernels: 57.9 us -> 56.7 us  [local(): pl.pallas_call(functools.partial(kernel, wide_size, narrow_size), out_sha...]
where the time goes in v3:
time: 60.3 us; the launch traced here: 60.1 us
  Pallas kernels  56.7 us (94%)
  local copies, waits for them, and re-layouts  2.77 us (5%)
  between operations  0.64 us (1%)
    pallas_call x1, Pallas kernels, local(): pl.pallas_call(functools.partial(kernel, wide_size, narrow_size), out_sha...  56.7 us
    unnamed x2, local copies, waits for them, and re-layouts  2.77 us

profile of v3, /device:TPU:0, one launch (start us, length us, event | category | flops | bytes accessed | tf_op | source)
XLA Modules:
  0.0 60.1 jit_solution(15864484524732760987)
XLA Ops:
  0.6 56.7 %shard_map.77 = (f32[16,128]{1,0:T(8,128)}, f32[128,128]{1,0:T(8,128)}) custom-call(s32[8,16]{1,0:T(8,128)} %bitcast.10, s32[1,16]{1,0:T(1,128)} %bitcast.11, f32[50,512]{1,0:T(8,128)} %source_hbm.1, f32[50,16384]{1,0:T(8,128)} %target_hbm.1, f32[16,128]{1,0:T(8,128)} %bitcast.8, f32[128,128]{1,0:T(8,128)} %bitcast.6), custom_call_target="tpu_custom_call" | custom-call | tf_op jit(solution)/shard_map/pallas_call | solution.py:441
  57.3 1.3 %copy.10 = f32[2048]{0:T(1024)} copy(f32[2048]{0:T(1024)} %bitcast.9) | data formatting | bytes 16384
  58.6 1.5 %copy.11 = f32[16384]{0:T(1024)} copy(f32[16384]{0:T(1024)} %bitcast.7) | data formatting | bytes 131072

commit v4 on v3

--- a/solution.py
+++ b/solution.py
@@ -15,6 +15,7 @@
 CHUNKS = 4
 SLABS = 16
 GROUP = 4
+HALVES = 2
 
 epsilon = 0.05
 very_low = -1e30
@@ -230,10 +231,12 @@
 
         lax.fori_loop(0, TILE // (slab * SLABS), one_group, 0)
 
-    def row_reduce():
+    half_count = row_count // HALVES
+
+    def row_reduce(part):
         def one_group(g, columns):
             for j in range(GROUP):
-                r = g * GROUP + j
+                r = part * half_count + g * GROUP + j
                 top = lane_peak[r]
                 peak = jnp.max(top, axis=1, keepdims=True)
                 mass = jnp.sum(lane_mass[r] * jnp.exp2(top - peak), axis=1, keepdims=True)
@@ -242,7 +245,7 @@
             return columns
 
         columns = lax.fori_loop(
-            0, row_count // GROUP, one_group, jnp.zeros((TILE, TILE), jnp.float32)
+            0, half_count // GROUP, one_group, jnp.zeros((TILE, TILE), jnp.float32)
         )
         return jnp.transpose(columns)
 
@@ -289,28 +292,34 @@
         lax.fori_loop(0, shard_tiles, one, 0)
     gather_leave()
 
-    def row_combine(step):
-        columns = row_reduce()
-        half = TILE // 2
-        row_send[step] = columns[0:row_count] + log2(columns[half : half + row_count])
+    def row_share(step, part):
+        columns = row_reduce(part)
+        first, half = part * half_count, TILE // 2
+        row_send[step, part] = columns[first : first + half_count] + log2(
+            columns[half + first : half + first + half_count]
+        )
         finish, _, _ = exchange(
             narrow_size,
             narrow_peer,
             at_narrow,
-            lambda to: row_send.at[step],
-            row_recv.at[step],
+            lambda to: row_send.at[step, part],
+            row_recv.at[step, part],
             narrow,
-            row_send_sem.at[step],
-            row_recv_sem.at[step],
-        )
-        row_recv[step, narrow] = row_send[step]
+            row_send_sem.at[step, part],
+            row_recv_sem.at[step, part],
+        )
+        row_recv[step, part, narrow] = row_send[step, part]
+        return finish
+
+    def row_combine(step, part, finish):
         finish()
-        parts = [row_recv[step, z] for z in range(narrow_size)]
+        parts = [row_recv[step, part, z] for z in range(narrow_size)]
         top = functools.reduce(jnp.maximum, parts)
         total = sum(jnp.exp2(p - top) for p in parts)
-        return log2(row_mass_ref[...]) - (top + log2(total))
-
-    def col_pass(step, row_values_ref):
+        rows = slice(part * half_count, (part + 1) * half_count)
+        row_out_ref[rows, :] = log2(row_mass_ref[rows, :]) - (top + log2(total))
+
+    def col_pass(step, row_values_ref, finishes):
         def one_tile(r, carry):
             values = jnp.transpose(
                 jnp.broadcast_to(row_values_ref[pl.ds(r, 1), :], (TILE, TILE))
@@ -352,7 +361,9 @@
             return carry
 
         col_peak[...] = jnp.full((col_count, TILE), very_low, jnp.float32)
-        lax.fori_loop(0, row_count, one_tile, 0)
+        for part in range(HALVES):
+            row_combine(step, part, finishes[part])
+            lax.fori_loop(part * half_count, (part + 1) * half_count, one_tile, 0)
 
         def rescale(r, carry):
             place = pl.ds(pl.multiple_of(r * K_MAX, K_MAX), K_MAX)
@@ -411,10 +422,12 @@
         return carry
 
     for step in range(ITERS):
-        if step > 0:
-            lax.fori_loop(0, row_count, row_pass, 0)
-        row_out_ref[...] = row_combine(step)
-        col_pass(step, row_out_ref)
+        finishes = []
+        for part in range(HALVES):
+            if step > 0:
+                lax.fori_loop(part * half_count, (part + 1) * half_count, row_pass, 0)
+            finishes.append(row_share(step, part))
+        col_pass(step, row_out_ref, finishes)
     row_out_ref[...] = potential_scale * (row_out_ref[...] + source_norm[...])
     col_out_ref[...] = potential_scale * (col_values[...] + target_norm[...])
 
@@ -461,8 +474,8 @@
             pltpu.VMEM((ITERS, wide_size, piece, TILE), f32),
             pltpu.VMEM((row_count, TILE, TILE), f32),
             pltpu.VMEM((row_count, TILE, TILE), f32),
-            pltpu.VMEM((ITERS, row_count, TILE), f32),
-            pltpu.VMEM((ITERS, narrow_size, row_count, TILE), f32),
+            pltpu.VMEM((ITERS, HALVES, row_count // HALVES, TILE), f32),
+            pltpu.VMEM((ITERS, HALVES, narrow_size, row_count // HALVES, TILE), f32),
             pltpu.VMEM((slots, TILE), f32),
             pltpu.VMEM((slots, TILE), f32),
             pltpu.VMEM((col_count, TILE), f32),
@@ -471,8 +484,8 @@
             dma((CHUNKS + 3,)),
             dma((narrow_size - 1,)),
             dma((narrow_size - 1,)),
-            dma((ITERS, narrow_size - 1)),
-            dma((ITERS, narrow_size - 1)),
+            dma((ITERS, HALVES, narrow_size - 1)),
+            dma((ITERS, HALVES, narrow_size - 1)),
             dma((ITERS, wide_size - 1)),
             dma((ITERS, wide_size - 1)),
             dma((ITERS, wide_size - 1)),

time: 60.3 us -> 58.6 us (0.972)
  Pallas kernels: 56.7 us -> 54.9 us
    pallas_call x1, Pallas kernels: 56.7 us -> 54.9 us  [local(): pl.pallas_call(functools.partial(kernel, wide_size, narrow_size), out_sha...]
where the time goes in v4:
time: 58.6 us; the launch traced here: 58.4 us
  Pallas kernels  54.9 us (94%)
  local copies, waits for them, and re-layouts  2.77 us (5%)
  between operations  0.64 us (1%)
    pallas_call x1, Pallas kernels, local(): pl.pallas_call(functools.partial(kernel, wide_size, narrow_size), out_sha...  54.9 us
    unnamed x2, local copies, waits for them, and re-layouts  2.77 us

profile of v4, /device:TPU:0, one launch (start us, length us, event | category | flops | bytes accessed | tf_op | source)
XLA Modules:
  0.0 58.4 jit_solution(14278725239312105883)
XLA Ops:
  0.6 54.9 %shard_map.77 = (f32[16,128]{1,0:T(8,128)}, f32[128,128]{1,0:T(8,128)}) custom-call(s32[8,16]{1,0:T(8,128)} %bitcast.10, s32[1,16]{1,0:T(1,128)} %bitcast.11, f32[50,512]{1,0:T(8,128)} %source_hbm.1, f32[50,16384]{1,0:T(8,128)} %target_hbm.1, f32[16,128]{1,0:T(8,128)} %bitcast.8, f32[128,128]{1,0:T(8,128)} %bitcast.6), custom_call_target="tpu_custom_call" | custom-call | tf_op jit(solution)/shard_map/pallas_call | solution.py:454
  55.6 1.3 %copy.10 = f32[2048]{0:T(1024)} copy(f32[2048]{0:T(1024)} %bitcast.9) | data formatting | bytes 16384
  56.9 1.5 %copy.11 = f32[16384]{0:T(1024)} copy(f32[16384]{0:T(1024)} %bitcast.7) | data formatting | bytes 131072
